TPU v7x, 256 devices: a whole 4x4x8 slice. The times are simulated.
256 devices in a mesh: grp: 8 (over z), tp: 32 (over y, x, core).
Axes of the slice: x: 4, y: 4, z: 8, core: 2. Of those that a mesh axis runs over, the one named last changes fastest.
Arguments:
- hidden_in: bfloat16 [512, 4096], P('grp'), may hold values from -6 to 6
- norm_gain: float32 [4096], replicated, may hold values from 0.25 to 1.75
- head_weight: bfloat16 [4096, 128256], P('grp', 'tp'), may hold values from -1 to 1
- ffn_act: bfloat16 [512, 14336], P('grp', 'tp'), may hold values from -6 to 6
- labels: int32 [512], P('grp'), may hold values from 0 to 128255
- lengths: int32 [64], P('grp'), may hold values from 1 to 8
- proj_hidden: bfloat16 [4096, 64], replicated, may hold values from -0.09375 to 0.09375
- proj_vocab: bfloat16 [128256, 64], P('tp'), may hold values from -6 to 6
- proj_ffn: bfloat16 [14336, 64], P('tp'), may hold values from -0.046875 to 0.046875
- proj_down: bfloat16 [4096, 64], replicated, may hold values from -6 to 6
- store: bfloat16 [65536, 8192], P('grp', 'tp'), may hold values from -0.0625 to 0.0625
Outputs:
- scores: float32 [64, 65536], P('tp', 'grp')
All inputs are finite; a program needn't handle non-finite values.
Results may differ from a plain program's by a relative error of at most 0.012.
Values may be sent and summed in bfloat16 or wider, within the bound.
No kernel may reach another device: no remote copies, remote signals or barrier semaphores. Data moves between devices by JAX's collectives and lax.ppermute only.
A program may use at most 64 MiB of HBM per device.

v0:
```python
import jax
import jax.numpy as jnp
from jax import lax
from jax.sharding import PartitionSpec as P

epsilon = 1e-05
highest = lax.Precision.HIGHEST


def sent_to_all(value, axis):
    copies = jnp.broadcast_to(value, (lax.axis_size(axis), *value.shape))
    return lax.all_to_all(copies, axis, split_axis=0, concat_axis=0, tiled=True)


def over_copies(value, axis):
    everything = sent_to_all(value, axis)
    return jnp.max(everything, axis=0)


def of_everyone(value, axis):
    everything = sent_to_all(value, axis)
    return jnp.sum(everything, axis=0)


def packed_total(arrays, axis):
    vector, at, outs = (jnp.concatenate([a.reshape(-1) for a in arrays]), 0, [])
    so_far = of_everyone(vector, axis)
    for a in arrays:
        outs.append(so_far[at : at + a.size].reshape(a.shape))
        at += a.size
    return tuple(outs)


def laid_out(tiles, dim):
    shape = list(tiles.shape[1:])
    shape[dim] *= tiles.shape[0]
    return jnp.moveaxis(tiles, 0, dim).reshape(shape)


def gather_directly(value, axis, dim):
    tiles = sent_to_all(value, axis)
    return laid_out(tiles, dim)


def cut_along(value, dim, length):
    before, after = (value.shape[:dim], value.shape[dim + 1 :])
    return jnp.moveaxis(value.reshape(*before, length, -1, *after), dim, 0)


def sent_and_summed(value, axis, dim):
    tiles = cut_along(value, dim, lax.axis_size(axis))
    arrived = lax.all_to_all(tiles, axis, split_axis=0, concat_axis=0, tiled=True)
    return arrived.sum(axis=0)


def fold_rows(pieces, high_part, low_part):
    contract = (((0,), (0,)), ((), ()))
    upper = lax.dot_general(pieces, high_part, contract, preferred_element_type=jnp.float32)
    return upper + lax.dot_general(pieces, low_part, contract, preferred_element_type=jnp.float32)


def per_device(
    hidden_in,
    norm_gain,
    head_weight,
    ffn_act,
    labels,
    lengths,
    proj_hidden,
    proj_vocab,
    proj_ffn,
    proj_down,
    store,
):
    token_count, model_width = hidden_in.shape
    query_here = lengths.shape[0]
    seq_span = token_count // query_here
    rows_owned, vocab_owned = head_weight.shape
    rank_size = proj_hidden.shape[1]
    group_index = lax.axis_index("grp")
    vocab_index = lax.axis_index("tp")
    wide_hidden = hidden_in.astype(jnp.float32)
    inverse = lax.rsqrt(jnp.mean(wide_hidden * wide_hidden, axis=1, keepdims=True) + epsilon)
    unit_hidden = wide_hidden * inverse
    normed = (norm_gain * unit_hidden).astype(jnp.bfloat16)
    gained_down = norm_gain[:, None] * proj_down.astype(jnp.float32)
    down_high = gained_down.astype(jnp.bfloat16)
    down_low = (gained_down - down_high.astype(jnp.float32)).astype(jnp.bfloat16)
    spread = lax.all_to_all(normed, "grp", split_axis=1, concat_axis=0, tiled=True)
    logits = lax.psum_scatter(
        jnp.dot(spread, head_weight, preferred_element_type=jnp.float32),
        "grp",
        scatter_dimension=0,
        tiled=True,
    )
    local_max = jnp.max(logits, axis=1)
    peak = over_copies(local_max, "tp")
    denominator = of_everyone(jnp.sum(jnp.exp(logits - peak[:, None]), axis=1), "tp")
    probs = jnp.exp(logits - peak[:, None]) / denominator[:, None]
    positions = lax.broadcasted_iota(jnp.int32, (token_count,), 0) % seq_span
    valid = positions < jnp.repeat(lengths, seq_span)
    vocab_ids = vocab_index * vocab_owned + lax.broadcasted_iota(jnp.int32, (1, vocab_owned), 1)
    onehot = (labels[:, None] == vocab_ids).astype(jnp.float32)
    grads = jnp.where(valid[:, None], probs - onehot, 0.0).astype(jnp.bfloat16)
    own_high = lax.dynamic_slice_in_dim(down_high, group_index * rows_owned, rows_owned, 0)
    own_low = lax.dynamic_slice_in_dim(down_low, group_index * rows_owned, rows_owned, 0)
    local_fold = fold_rows(head_weight, own_high, own_low)
    folded_sum = lax.psum(local_fold, "grp")
    down_sum = jnp.dot(grads.astype(jnp.float32), folded_sum, precision=highest)
    head_side = jnp.dot(grads, proj_vocab, preferred_element_type=jnp.float32)
    label_dot = jnp.sum(grads.astype(jnp.float32) * logits, axis=1)
    ffn_side = jnp.dot(ffn_act, proj_ffn, preferred_element_type=jnp.float32)
    head_side, down_sum, label_dot, ffn_side = packed_total(
        (head_side, down_sum, label_dot, ffn_side), "tp"
    )
    hidden_side = jnp.dot(normed, proj_hidden, preferred_element_type=jnp.float32)
    unit_down = jnp.dot(unit_hidden, proj_down.astype(jnp.float32), precision=highest)
    down_side = inverse * (down_sum - (label_dot / model_width)[:, None] * unit_down)
    shaped = (query_here, seq_span, rank_size)
    first_outer = jnp.einsum("spa,spb->sab", hidden_side.reshape(shaped), head_side.reshape(shaped))
    second_outer = jnp.einsum("spa,spb->sab", ffn_side.reshape(shaped), down_side.reshape(shaped))
    queries = jnp.concatenate(
        [first_outer.reshape(query_here, -1), second_outer.reshape(query_here, -1)], axis=1
    ).astype(jnp.bfloat16)
    feature_owned = store.shape[1]
    own_queries = lax.dynamic_slice_in_dim(queries, vocab_index * feature_owned, feature_owned, 1)
    every_query = gather_directly(own_queries, "grp", 0)
    return sent_and_summed(
        lax.dot_general(
            every_query, store, (((1,), (1,)), ((), ())), preferred_element_type=jnp.float32
        ),
        "tp",
        0,
    )


def solution(mesh):
    return jax.shard_map(
        per_device,
        mesh=mesh,
        in_specs=(
            P("grp", None),
            P(),
            P("grp", "tp"),
            P("grp", "tp"),
            P("grp"),
            P("grp"),
            P(),
            P("tp", None),
            P("tp", None),
            P(),
            P("grp", "tp"),
        ),
        out_specs=P("tp", "grp"),
        check_vma=False,
    )
```

profile of v0, /device:TPU:1, one launch (start us, length us, event | category | flops | bytes accessed | tf_op | source)
XLA Modules:
  0.0 308.6 jit_solution(2016261024021584329)
XLA Ops:
  6.5 1.3 fusion.10
  7.9 1.2 fusion.9
  9.1 24.9 %all_to_all.47 = bf16[64,8,512]{2,0,1:T(8,128)(2,1)S(1)} all-to-all(bf16[64,8,512]{2,0,1:T(8,128)(2,1)S(1)} %bitcast.38), channel_id=1, replica_groups=mesh['grp'=8,'tp'=32] {'grp'}, dimensions={1} | all-to-all | bytes 1048576 | tf_op jit(solution)/shard_map/all_to_all | solution.py:89
  34.1 7.8 %fusion.25 = f32[512,4008]{1,0:T(8,128)} fusion(bf16[512,512]{1,0:T(8,128)(2,1)S(1)} %bitcast.37, bf16[512,4008]{0,1:T(8,128)(2,1)} %param.13), kind=kOutput, calls=%fused_computation.42 | convolution fusion | flops 2101346304 | bytes 12836864 | tf_op jit(solution)/shard_map/dot_general | solution.py:91
  42.0 1.0 copy-done.3
  43.1 3.7 %fusion.17 = f32[64,4008]{1,0:T(8,128)S(1)} fusion(bf16[512,4008]{0,1:T(8,128)(2,1)} %param.13, bf16[4096,64]{0,1:T(8,128)(2,1)S(1)} %get-tuple-element.8, s32[]{:T(128)S(6)} %select_n.24), kind=kOutput, calls=%fused_computation.30 | convolution fusion | flops 262668288 | bytes 5195780 | tf_op jit(solution)/shard_map/dot_general | solution.py:58
  46.8 2.3 fusion
  49.5 85.5 %reduce-scatter.2.cloned.1.call-done = f32[64,4008]{1,0:T(8,128)} async-done(((f32[512,4008]{1,0:T(8,128)}), f32[64,4008]{1,0:T(8,128)}) %reduce-scatter.2.cloned.1.call-update) | async-done | bytes 1026064 | tf_op jit(solution)/shard_map/reduce_scatter | solution.py:90
  134.9 1.4 reduce_max.18
  136.3 0.6 broadcast_in_dim.38
  136.9 7.6 %all-to-all-start.1 = ((f32[32,1,64]{2,1,0:T(1,128)}), f32[32,1,64]{2,1,0:T(1,128)S(1)}, u32[]{:S(2)}, u32[]{:S(2)}) async-start(f32[32,1,64]{2,1,0:T(1,128)} %broadcast_in_dim.38), calls=%async_computation.2 | async-start | bytes 32768 | tf_op jit(solution)/shard_map/all_to_all | solution.py:12
  144.5 6.9 %all-to-all-done.1 = f32[32,1,64]{2,1,0:T(1,128)S(1)} async-done(((f32[32,1,64]{2,1,0:T(1,128)}), f32[32,1,64]{2,1,0:T(1,128)S(1)}, u32[]{:S(2)}, u32[]{:S(2)}) %all-to-all-start.1) | async-done | bytes 8224 | tf_op jit(solution)/shard_map/all_to_all | solution.py:12
  151.4 1.5 fusion.11
  153.0 0.6 broadcast_in_dim.39
  153.6 4.1 %all-to-all-start.2 = ((f32[32,1,64]{2,1,0:T(1,128)}), f32[32,1,64]{2,1,0:T(1,128)S(1)}, u32[]{:S(2)}, u32[]{:S(2)}) async-start(f32[32,1,64]{2,1,0:T(1,128)} %broadcast_in_dim.39), calls=%async_computation.3 | async-start | bytes 32768 | tf_op jit(solution)/shard_map/all_to_all | solution.py:12
  157.8 6.9 %all-to-all-done.2 = f32[32,1,64]{2,1,0:T(1,128)S(1)} async-done(((f32[32,1,64]{2,1,0:T(1,128)}), f32[32,1,64]{2,1,0:T(1,128)S(1)}, u32[]{:S(2)}, u32[]{:S(2)}) %all-to-all-start.2) | async-done | bytes 8224 | tf_op jit(solution)/shard_map/all_to_all | solution.py:12
  164.8 1.8 multiply_reduce_fusion
  166.6 0.3 fusion.26
  166.9 40.7 %all-reduce.2.cloned.1.call-done = f32[4008,64]{0,1:T(8,128)} async-done(((f32[4008,64]{0,1:T(8,128)}), f32[4008,64]{0,1:T(8,128)}) %all-reduce.2.cloned.1.call-update) | async-done | bytes 1026064 | tf_op jit(solution)/shard_map/psum | solution.py:108
  207.6 1.9 fusion.27
  209.7 2.0 broadcast_in_dim.41
  211.6 11.9 %all-to-all-start.3 = ((f32[32,1,12352]{2,1,0:T(1,128)}), f32[32,1,12352]{2,1,0:T(1,128)S(1)}, u32[]{:S(2)}, u32[]{:S(2)}) async-start(f32[32,1,12352]{2,1,0:T(1,128)} %broadcast_in_dim.41), calls=%async_computation.4 | async-start | bytes 3178496 | tf_op jit(solution)/shard_map/all_to_all | solution.py:12
  223.6 22.4 %all-to-all-done.3 = f32[32,1,12352]{2,1,0:T(1,128)S(1)} async-done(((f32[32,1,12352]{2,1,0:T(1,128)}), f32[32,1,12352]{2,1,0:T(1,128)S(1)}, u32[]{:S(2)}, u32[]{:S(2)}) %all-to-all-start.3) | async-done | bytes 1581088 | tf_op jit(solution)/shard_map/all_to_all | solution.py:12
  246.0 0.9 reduce_sum.58
  247.1 0.6 convolution_convert_fusion.1
  248.0 1.8 fusion.8
  249.8 0.2 fusion.29
  250.3 10.6 %all_to_all.48 = bf16[8,8,256]{2,1,0:T(8,128)(2,1)S(1)} all-to-all(bf16[8,8,256]{2,1,0:T(8,128)(2,1)S(1)} %broadcast_in_dim.42), channel_id=1, replica_groups=mesh['grp'=8,'tp'=32] {'grp'}, dimensions={0} | all-to-all | bytes 65536 | tf_op jit(solution)/shard_map/all_to_all | solution.py:12
  260.8 3.6 %fusion.1 = f32[32,2,8192]{2,0,1:T(8,128)S(1)} fusion(bf16[8192,256]{1,0:T(8,128)(2,1)} %param.21, bf16[32,2,256]{2,1,0:T(2,128)(2,1)S(1)} %dot_general.45), kind=kOutput, calls=%fused_computation.2 | convolution fusion | flops 268435456 | bytes 6324224 | tf_op jit(solution)/shard_map/dot_general | solution.py:129
  264.4 1.6 copy.26
  266.0 34.4 %all_to_all.49 = f32[32,2,8192]{2,1,0:T(2,128)S(1)} all-to-all(f32[32,2,8192]{2,1,0:T(2,128)S(1)} %copy.26), channel_id=1, replica_groups=mesh['grp'=8,'tp'=32] {'tp'}, dimensions={0} | all-to-all | bytes 4194304 | tf_op jit(solution)/shard_map/all_to_all | solution.py:52
  300.4 1.4 reduce_sum.59
  (48 shorter events, 1.7 us)
Async XLA Ops:
  6.5 240.6 %copy-start = (bf16[4096,64]{0,1:T(8,128)(2,1)S(1)}, bf16[4096,64]{0,1:T(8,128)(2,1)}, u32[]{:S(2)}) copy-start(bf16[4096,64]{0,1:T(8,128)(2,1)} %param.17) | copy-start | bytes 1572868
  6.5 128.4 %reduce-scatter.2.cloned.1.call-start = ((), (), s32[]{:S(2)}) async-start(), calls=%async_computation.7 | async-start | bytes 9437184 | tf_op jit(solution)/shard_map/reduce_scatter | solution.py:90
  41.9 1.0 copy-start.3
  41.9 1.0 copy-start.5
  41.9 165.7 %all-reduce.2.cloned.1.call-start = ((), (), s32[]{:S(2)}) async-start(), calls=%async_computation.8 | async-start | bytes 2097152 | tf_op jit(solution)/shard_map/psum | solution.py:108
  42.9 3.9 %copy-start.1 = (bf16[512,4008]{0,1:T(8,128)(2,1)S(1)}, bf16[512,4008]{0,1:T(8,128)(2,1)}, u32[]{:S(2)}) copy-start(bf16[512,4008]{0,1:T(8,128)(2,1)} %param.13) | copy-start | bytes 12312580
  46.7 2.4 copy-start.9
  46.7 2.6 copy-start.6
  46.8 2.6 copy-start.7
  46.8 118.0 %copy-start.8 = (s32[64]{0:T(128)S(1)}, s32[64]{0:T(128)}, u32[]{:S(2)}) copy-start(s32[64]{0:T(128)} %param.15) | copy-start | bytes 772
  49.1 117.4 %copy-start.4 = (bf16[4008,64]{0,1:T(8,128)(2,1)S(1)}, bf16[4008,64]{0,1:T(8,128)(2,1)}, u32[]{:S(2)}) copy-start(bf16[4008,64]{0,1:T(8,128)(2,1)} %param.18) | copy-start | bytes 1539076
  136.9 14.5 %all-to-all-start.1 = ((f32[32,1,64]{2,1,0:T(1,128)}), f32[32,1,64]{2,1,0:T(1,128)S(1)}, u32[]{:S(2)}, u32[]{:S(2)}) async-start(f32[32,1,64]{2,1,0:T(1,128)} %broadcast_in_dim.38), calls=%async_computation.2 | async-start | bytes 32768 | tf_op jit(solution)/shard_map/all_to_all | solution.py:12
  153.6 11.1 %all-to-all-start.2 = ((f32[32,1,64]{2,1,0:T(1,128)}), f32[32,1,64]{2,1,0:T(1,128)S(1)}, u32[]{:S(2)}, u32[]{:S(2)}) async-start(f32[32,1,64]{2,1,0:T(1,128)} %broadcast_in_dim.39), calls=%async_computation.3 | async-start | bytes 32768 | tf_op jit(solution)/shard_map/all_to_all | solution.py:12
  209.5 38.5 %copy-start.2 = (bf16[64,4096]{1,0:T(8,128)(2,1)S(1)}, bf16[64,4096]{1,0:T(8,128)(2,1)}, u32[]{:S(2)}) copy-start(bf16[64,4096]{1,0:T(8,128)(2,1)} %param.11) | copy-start | bytes 1572868
  211.6 34.4 %all-to-all-start.3 = ((f32[32,1,12352]{2,1,0:T(1,128)}), f32[32,1,12352]{2,1,0:T(1,128)S(1)}, u32[]{:S(2)}, u32[]{:S(2)}) async-start(f32[32,1,12352]{2,1,0:T(1,128)} %broadcast_in_dim.41), calls=%async_computation.4 | async-start | bytes 3178496 | tf_op jit(solution)/shard_map/all_to_all | solution.py:12
Sparse Core Ops, SparseCore 0:
  42.0 92.8 reduce-scatter.1
  137.3 70.2 all-reduce.1
where the time goes:
time: 309 us
  waiting for transfers between devices  162 us (52%)
  blocking collectives  69.8 us (23%)
  starting transfers between devices  23.7 us (8%)
  matrix products  22.3 us (7%)
  between operations  13.7 us (4%)
  other arithmetic  9.72 us (3%)
  local copies, waits for them, and re-layouts  7.04 us (2%)
    reduce_scatter x1, waiting for transfers between devices, per_device(): lax.psum_scatter(jnp.dot(spread, head_weight, preferred_element_type=jnp....  85.5 us
    psum x1, waiting for transfers between devices, per_device(): folded_sum = lax.psum(local_fold, 'grp')  40.7 us
    all_to_all x3, waiting for transfers between devices, sent_to_all(): return lax.all_to_all(copies, axis, split_axis=0, concat_axis=0, tiled=True)  36.2 us
    all_to_all x1, blocking collectives, sent_and_summed(): lax.all_to_all(tiles, axis, split_axis=0, concat_axis=0, tiled=True)  34.4 us
    all_to_all x1, blocking collectives, per_device(): lax.all_to_all(normed, 'grp', split_axis=1, concat_axis=0, tiled=True)  24.9 us
    all_to_all x3, starting transfers between devices, sent_to_all(): return lax.all_to_all(copies, axis, split_axis=0, concat_axis=0, tiled=True)  23.6 us
    all_to_all x1, blocking collectives, sent_to_all(): return lax.all_to_all(copies, axis, split_axis=0, concat_axis=0, tiled=True)  10.6 us
    dot_general x1, matrix products, per_device(): jnp.dot(spread, head_weight, preferred_element_type=jnp.float32)  7.81 us
  transfers between devices with their start and end apart: 5, of which 5 were waited for; matrix products, arithmetic and copies ran while one was open for 4% of the time, Pallas kernels for 0%

commit v1 on v0

--- a/solution.py
+++ b/solution.py
@@ -5,6 +5,11 @@
 
 epsilon = 1e-05
 highest = lax.Precision.HIGHEST
+
+
+def add_all(x, axis):
+    blocks = lax.all_gather(x, axis)
+    return jnp.sum(blocks, axis=0)
 
 
 def sent_to_all(value, axis):
@@ -105,7 +110,7 @@
     own_high = lax.dynamic_slice_in_dim(down_high, group_index * rows_owned, rows_owned, 0)
     own_low = lax.dynamic_slice_in_dim(down_low, group_index * rows_owned, rows_owned, 0)
     local_fold = fold_rows(head_weight, own_high, own_low)
-    folded_sum = lax.psum(local_fold, "grp")
+    folded_sum = add_all(local_fold, "grp")
     down_sum = jnp.dot(grads.astype(jnp.float32), folded_sum, precision=highest)
     head_side = jnp.dot(grads, proj_vocab, preferred_element_type=jnp.float32)
     label_dot = jnp.sum(grads.astype(jnp.float32) * logits, axis=1)

time: 309 us -> 333 us (1.078)
  waiting for transfers between devices: 162 us -> 186 us
  starting transfers between devices: 23.7 us -> 19.5 us
  other arithmetic: 9.72 us -> 13.5 us
    all_gather x0 -> x1, waiting for transfers between devices: none -> 71.5 us  [add_all(): blocks = lax.all_gather(x, axis)]
    psum x1 -> x0, waiting for transfers between devices: 40.7 us -> none  [per_device(): folded_sum = lax.psum(local_fold, 'grp')]
    all_to_all x3, waiting for transfers between devices: 36.2 us -> 29.3 us  [sent_to_all(): return lax.all_to_all(copies, axis, split_axis=0, concat_axis=0, tiled=True)]
    reduce_sum x0 -> x1, other arithmetic: none -> 5.04 us  [add_all(): return jnp.sum(blocks, axis=0)]
    all_to_all x3, starting transfers between devices: 23.6 us -> 19.4 us  [sent_to_all(): return lax.all_to_all(copies, axis, split_axis=0, concat_axis=0, tiled=True)]
  transfers between devices with their start and end apart: 5 -> 5, of which waited for: 5 -> 4; matrix products, arithmetic and copies ran while one was open for 4% -> 5% of each run, Pallas kernels for 0% -> 0%
where the time goes in v1:
time: 333 us; the launch traced here: 332 us
  waiting for transfers between devices  186 us (56%)
  blocking collectives  70 us (21%)
  matrix products  22.3 us (7%)
  starting transfers between devices  19.5 us (6%)
  between operations  13.7 us (4%)
  other arithmetic  13.5 us (4%)
  local copies, waits for them, and re-layouts  7.04 us (2%)
    reduce_scatter x1, waiting for transfers between devices, per_device(): lax.psum_scatter(jnp.dot(spread, head_weight, preferred_element_type=jnp....  85.4 us
    all_gather x1, waiting for transfers between devices, add_all(): blocks = lax.all_gather(x, axis)  71.5 us
    all_to_all x1, blocking collectives, sent_and_summed(): lax.all_to_all(tiles, axis, split_axis=0, concat_axis=0, tiled=True)  34.4 us
    all_to_all x3, waiting for transfers between devices, sent_to_all(): return lax.all_to_all(copies, axis, split_axis=0, concat_axis=0, tiled=True)  29.3 us
    all_to_all x1, blocking collectives, per_device(): lax.all_to_all(normed, 'grp', split_axis=1, concat_axis=0, tiled=True)  24.9 us
    all_to_all x3, starting transfers between devices, sent_to_all(): return lax.all_to_all(copies, axis, split_axis=0, concat_axis=0, tiled=True)  19.4 us
    all_to_all x1, blocking collectives, sent_to_all(): return lax.all_to_all(copies, axis, split_axis=0, concat_axis=0, tiled=True)  10.7 us
    dot_general x1, matrix products, per_device(): jnp.dot(spread, head_weight, preferred_element_type=jnp.float32)  7.8 us
  transfers between devices with their start and end apart: 5, of which 4 were waited for; matrix products, arithmetic and copies ran while one was open for 5% of the time, Pallas kernels for 0%

profile of v1, /device:TPU:1, one launch (start us, length us, event | category | flops | bytes accessed | tf_op | source)
XLA Modules:
  0.0 332.3 jit_solution(9030924463216319571)
XLA Ops:
  6.5 1.3 fusion.10
  7.9 1.2 fusion.9
  9.1 24.9 %all_to_all.47 = bf16[64,8,512]{2,0,1:T(8,128)(2,1)S(1)} all-to-all(bf16[64,8,512]{2,0,1:T(8,128)(2,1)S(1)} %bitcast.40), channel_id=1, replica_groups=mesh['grp'=8,'tp'=32] {'grp'}, dimensions={1} | all-to-all | bytes 1048576 | tf_op jit(solution)/shard_map/all_to_all | solution.py:94
  34.1 7.8 %fusion.25 = f32[512,4008]{1,0:T(8,128)} fusion(bf16[512,512]{1,0:T(8,128)(2,1)S(1)} %bitcast.39, bf16[512,4008]{0,1:T(8,128)(2,1)} %param.13), kind=kOutput, calls=%fused_computation.42 | convolution fusion | flops 2101346304 | bytes 12836864 | tf_op jit(solution)/shard_map/dot_general | solution.py:96
  41.9 1.0 copy-done.4
  43.0 3.7 %fusion.17 = f32[64,4008]{1,0:T(8,128)S(1)} fusion(bf16[512,4008]{0,1:T(8,128)(2,1)} %param.13, bf16[4096,64]{0,1:T(8,128)(2,1)S(1)} %get-tuple-element.8, s32[]{:T(128)S(6)} %select_n.24), kind=kOutput, calls=%fused_computation.30 | convolution fusion | flops 262668288 | bytes 5195780 | tf_op jit(solution)/shard_map/dot_general | solution.py:63
  46.8 2.4 fusion
  49.5 85.4 %reduce-scatter.2.cloned.1.call-done = f32[64,4008]{1,0:T(8,128)} async-done(((f32[512,4008]{1,0:T(8,128)}), f32[64,4008]{1,0:T(8,128)}) %reduce-scatter.2.cloned.1.call-update) | async-done | bytes 1026064 | tf_op jit(solution)/shard_map/reduce_scatter | solution.py:95
  134.9 1.4 reduce_max.18
  136.3 0.6 broadcast_in_dim.38
  136.9 7.6 %all-to-all-start.1 = ((f32[32,1,64]{2,1,0:T(1,128)}), f32[32,1,64]{2,1,0:T(1,128)S(1)}, u32[]{:S(2)}, u32[]{:S(2)}) async-start(f32[32,1,64]{2,1,0:T(1,128)} %broadcast_in_dim.38), calls=%async_computation.2 | async-start | bytes 32768 | tf_op jit(solution)/shard_map/all_to_all | solution.py:17
  144.5 6.9 %all-to-all-done.1 = f32[32,1,64]{2,1,0:T(1,128)S(1)} async-done(((f32[32,1,64]{2,1,0:T(1,128)}), f32[32,1,64]{2,1,0:T(1,128)S(1)}, u32[]{:S(2)}, u32[]{:S(2)}) %all-to-all-start.1) | async-done | bytes 8224 | tf_op jit(solution)/shard_map/all_to_all | solution.py:17
  151.4 1.5 fusion.11
  153.0 0.6 broadcast_in_dim.39
  153.6 4.1 %all-to-all-start.2 = ((f32[32,1,64]{2,1,0:T(1,128)}), f32[32,1,64]{2,1,0:T(1,128)S(1)}, u32[]{:S(2)}, u32[]{:S(2)}) async-start(f32[32,1,64]{2,1,0:T(1,128)} %broadcast_in_dim.39), calls=%async_computation.3 | async-start | bytes 32768 | tf_op jit(solution)/shard_map/all_to_all | solution.py:17
  157.8 71.5 %all-gather.4.cloned.1.call-done = f32[8,4008,64]{1,2,0:T(8,128)} async-done(((f32[1,4008,64]{1,2,0:T(8,128)}), f32[8,4008,64]{1,2,0:T(8,128)}) %all-gather.4.cloned.1.call-update) | async-done | bytes 8208400 | tf_op jit(solution)/shard_map/all_gather | solution.py:11
  229.3 5.0 %reduce_sum.66 = f32[4008,64]{0,1:T(8,128)} reduce(f32[8,4008,64]{1,2,0:T(8,128)} %all-gather.4.cloned.1.call-done, f32[]{:T(128)} %constant.15.clone.1), dimensions={0}, to_apply=%region_6.7 | reduce | flops 1795584 | bytes 9234436 | tf_op jit(solution)/shard_map/reduce_sum | solution.py:12
  234.4 0.5 multiply_reduce_fusion
  235.0 0.3 fusion.26
  235.3 1.9 fusion.27
  237.4 2.0 broadcast_in_dim.41
  239.3 7.7 %all-to-all-start.3 = ((f32[32,1,12352]{2,1,0:T(1,128)}), f32[32,1,12352]{2,1,0:T(1,128)S(1)}, u32[]{:S(2)}, u32[]{:S(2)}) async-start(f32[32,1,12352]{2,1,0:T(1,128)} %broadcast_in_dim.41), calls=%async_computation.4 | async-start | bytes 3178496 | tf_op jit(solution)/shard_map/all_to_all | solution.py:17
  247.1 22.4 %all-to-all-done.3 = f32[32,1,12352]{2,1,0:T(1,128)S(1)} async-done(((f32[32,1,12352]{2,1,0:T(1,128)}), f32[32,1,12352]{2,1,0:T(1,128)S(1)}, u32[]{:S(2)}, u32[]{:S(2)}) %all-to-all-start.3) | async-done | bytes 1581088 | tf_op jit(solution)/shard_map/all_to_all | solution.py:17
  269.5 0.9 reduce_sum.68
  270.6 0.6 convolution_convert_fusion.1
  271.5 1.8 fusion.8
  273.3 0.2 fusion.29
  273.8 10.7 %all_to_all.48 = bf16[8,8,256]{2,1,0:T(8,128)(2,1)S(1)} all-to-all(bf16[8,8,256]{2,1,0:T(8,128)(2,1)S(1)} %broadcast_in_dim.42), channel_id=1, replica_groups=mesh['grp'=8,'tp'=32] {'grp'}, dimensions={0} | all-to-all | bytes 65536 | tf_op jit(solution)/shard_map/all_to_all | solution.py:17
  284.5 3.6 %fusion.1 = f32[32,2,8192]{2,0,1:T(8,128)S(1)} fusion(bf16[8192,256]{1,0:T(8,128)(2,1)} %param.21, bf16[32,2,256]{2,1,0:T(2,128)(2,1)S(1)} %dot_general.45), kind=kOutput, calls=%fused_computation.2 | convolution fusion | flops 268435456 | bytes 6324224 | tf_op jit(solution)/shard_map/dot_general | solution.py:134
  288.0 1.6 copy.26
  289.7 34.4 %all_to_all.49 = f32[32,2,8192]{2,1,0:T(2,128)S(1)} all-to-all(f32[32,2,8192]{2,1,0:T(2,128)S(1)} %copy.26), channel_id=1, replica_groups=mesh['grp'=8,'tp'=32] {'tp'}, dimensions={0} | all-to-all | bytes 4194304 | tf_op jit(solution)/shard_map/all_to_all | solution.py:57
  324.0 1.4 reduce_sum.69
  (51 shorter events, 1.7 us)
Async XLA Ops:
  6.5 264.1 %copy-start = (bf16[4096,64]{0,1:T(8,128)(2,1)S(1)}, bf16[4096,64]{0,1:T(8,128)(2,1)}, u32[]{:S(2)}) copy-start(bf16[4096,64]{0,1:T(8,128)(2,1)} %param.17) | copy-start | bytes 1572868
  6.5 128.4 %reduce-scatter.2.cloned.1.call-start = ((), (), s32[]{:S(2)}) async-start(), calls=%async_computation.7 | async-start | bytes 9437184 | tf_op jit(solution)/shard_map/reduce_scatter | solution.py:95
  41.9 1.0 copy-start.4
  41.9 1.0 copy-start.6
  41.9 187.5 %all-gather.4.cloned.1.call-start = ((), (), s32[]{:S(2)}) async-start(), calls=%async_computation.8 | async-start | bytes 9437184 | tf_op jit(solution)/shard_map/all_gather | solution.py:11
  42.9 3.9 %copy-start.1 = (bf16[512,4008]{0,1:T(8,128)(2,1)S(1)}, bf16[512,4008]{0,1:T(8,128)(2,1)}, u32[]{:S(2)}) copy-start(bf16[512,4008]{0,1:T(8,128)(2,1)} %param.13) | copy-start | bytes 12312580
  46.7 2.5 copy-start.10
  46.7 2.6 copy-start.7
  46.7 2.6 copy-start.8
  136.9 14.5 %all-to-all-start.1 = ((f32[32,1,64]{2,1,0:T(1,128)}), f32[32,1,64]{2,1,0:T(1,128)S(1)}, u32[]{:S(2)}, u32[]{:S(2)}) async-start(f32[32,1,64]{2,1,0:T(1,128)} %broadcast_in_dim.38), calls=%async_computation.2 | async-start | bytes 32768 | tf_op jit(solution)/shard_map/all_to_all | solution.py:17
  153.6 80.8 %all-to-all-start.2 = ((f32[32,1,64]{2,1,0:T(1,128)}), f32[32,1,64]{2,1,0:T(1,128)S(1)}, u32[]{:S(2)}, u32[]{:S(2)}) async-start(f32[32,1,64]{2,1,0:T(1,128)} %broadcast_in_dim.39), calls=%async_computation.3 | async-start | bytes 32768 | tf_op jit(solution)/shard_map/all_to_all | solution.py:17
  157.8 76.6 %copy-start.2 = (f32[64,4008]{1,0:T(8,128)S(1)}, f32[64,4008]{1,0:T(8,128)}, u32[]{:S(2)}) copy-start(f32[64,4008]{1,0:T(8,128)} %reduce-scatter.2.cloned.1.call-done) | copy-start | bytes 3078148
  157.8 76.6 %copy-start.9 = (s32[64]{0:T(128)S(1)}, s32[64]{0:T(128)}, u32[]{:S(2)}) copy-start(s32[64]{0:T(128)} %param.15) | copy-start | bytes 772
  157.8 77.1 %copy-start.5 = (bf16[4008,64]{0,1:T(8,128)(2,1)S(1)}, bf16[4008,64]{0,1:T(8,128)(2,1)}, u32[]{:S(2)}) copy-start(bf16[4008,64]{0,1:T(8,128)(2,1)} %param.18) | copy-start | bytes 1539076
  237.2 34.3 %copy-start.3 = (bf16[64,4096]{1,0:T(8,128)(2,1)S(1)}, bf16[64,4096]{1,0:T(8,128)(2,1)}, u32[]{:S(2)}) copy-start(bf16[64,4096]{1,0:T(8,128)(2,1)} %param.11) | copy-start | bytes 1572868
  239.3 30.2 %all-to-all-start.3 = ((f32[32,1,12352]{2,1,0:T(1,128)}), f32[32,1,12352]{2,1,0:T(1,128)S(1)}, u32[]{:S(2)}, u32[]{:S(2)}) async-start(f32[32,1,12352]{2,1,0:T(1,128)} %broadcast_in_dim.41), calls=%async_computation.4 | async-start | bytes 3178496 | tf_op jit(solution)/shard_map/all_to_all | solution.py:17
Sparse Core Ops, SparseCore 0:
  42.0 92.8 reduce-scatter.1
  136.7 92.5 all-gather.3
